TPU v7x, 32 devices: a whole 2x2x4 slice. The times are simulated.
32 devices in a mesh: groups: 2 (over y), dp: 4 (over z), tensor: 4 (over x, core).
Axes of the slice: x: 2, y: 2, z: 4, core: 2. Of those that a mesh axis runs over, the one named last changes fastest.
Arguments:
- feature_cache: bfloat16 [512, 8, 3, 8192], P(('groups', 'dp'), None, None, 'tensor'), parts along dimension 0
- owner_ids: int32 [512, 1], P(('groups', 'dp')), parts along dimension 0, may hold values from 0 to 3; in each aligned block of 64 rows (0 to 63, 64 to 127, ...) at most 24 rows name the same one
- slot_ids: int32 [512], P(('groups', 'dp')), parts along dimension 0, may hold values from 0 to 63
- live_tokens: int32 [512], P(('groups', 'dp')), parts along dimension 0, may hold values from 1 to 8
- tap_gain: float32 [3, 8192], P(None, 'tensor'), may hold values from 0.1 to 1.9
- key_cotangent: bfloat16 [4096, 1024], P(('groups', 'dp'), 'tensor'), parts along dimension 0, may hold values from -0.1875 to 0.1875
- value_cotangent: bfloat16 [4096, 1024], P(('groups', 'dp'), 'tensor'), parts along dimension 0, may hold values from -0.1875 to 0.1875
Outputs:
- kv_gradient: float32 [4096, 8192], P(('groups', 'dp'), 'tensor'), parts along dimension 0
There are 2 independent parts, one for each index of `groups`. A program takes and returns all parts, laid end to end along the dimension named above; an argument that names none is the same for every part. Nothing has to cross between parts.
Inputs may be any that keep to these rules, and one draw needn't show every extreme that they name: `owner_ids`: among the 64 entries of one device's list, no owner is named more than 24 times, a bound that some block reaches.
All inputs are finite; a program needn't handle non-finite values.
Results may differ from a plain program's by a relative error of at most 0.009.
Values may be sent and summed in bfloat16 or wider, within the bound.
A program may use at most 128 MiB of HBM per device.

v0:
```python
import jax
import jax.numpy as jnp
from jax import lax
from jax.sharding import PartitionSpec as P

D = 8192


epsilon = 1e-06


def joined_cotangents(key_rows, value_rows):
    key_all, value_all = (
        lax.all_gather(key_rows, "tensor", axis=1, tiled=True),
        lax.all_gather(value_rows, "tensor", axis=1, tiled=True),
    )
    return jnp.concatenate([key_all, value_all], axis=1)


def live_where(live_counts, block_len):
    offsets = jnp.arange(block_len, dtype=jnp.int32)
    return offsets[None, :] < live_counts[:, None]


def body(feature_cache, owner_ids, slot_ids, live_tokens, tap_gain, key_cotangent, value_cotangent):
    owners = lax.axis_size("dp")
    listed = slot_ids.shape[0]
    block_len = feature_cache.shape[1]
    columns = feature_cache.shape[3]
    capacity = max(2, 3 * listed // (2 * owners))
    target = owner_ids[:, 0]
    matches = (target[:, None] == jnp.arange(owners, dtype=jnp.int32)[None, :]).astype(jnp.int32)
    before = jnp.cumsum(matches, axis=0) - matches
    order_rank = jnp.sum(before * matches, axis=1)
    position = target * capacity + order_rank
    pairs = jnp.stack([slot_ids, live_tokens], axis=1)
    request = (
        jnp.zeros((owners * capacity, 2), jnp.int32)
        .at[position]
        .set(pairs)
        .reshape(owners, capacity, 2)
    )
    requested = lax.all_to_all(request, "dp", split_axis=0, concat_axis=0, tiled=True)
    slots = requested[..., 0].reshape(-1)
    live_mask = live_where(requested[..., 1].reshape(-1), block_len)
    blocks = jnp.take(feature_cache, slots, axis=0)
    blocks = jnp.where(live_mask[:, :, None, None], blocks, jnp.zeros_like(blocks))
    shaped = blocks.reshape(requested.shape[:2] + blocks.shape[1:])
    arrived = lax.all_to_all(shaped, "dp", split_axis=0, concat_axis=0, tiled=True)
    picked = arrived.reshape((owners * capacity,) + arrived.shape[2:])[position]
    floats = picked.astype(jnp.float32)
    squares = jnp.sum(floats * floats, axis=-1)
    summed = lax.psum(squares, "tensor")
    inverse_rms = lax.rsqrt(summed / D + epsilon)
    united = jnp.sum(floats * inverse_rms[..., None] * tap_gain, axis=2).astype(jnp.bfloat16)
    cotangent = joined_cotangents(key_cotangent, value_cotangent)
    united = united.reshape(-1, columns)
    return lax.psum_scatter(
        lax.dot_general(
            cotangent, united, (((0,), (0,)), ((), ())), preferred_element_type=jnp.float32
        ).astype(jnp.bfloat16),
        "dp",
        scatter_dimension=0,
        tiled=True,
    ).astype(jnp.float32)


def solution(mesh):
    in_specs = (
        P(("groups", "dp"), None, None, "tensor"),
        P(("groups", "dp"), None),
        P(("groups", "dp")),
        P(("groups", "dp")),
        P(None, "tensor"),
        P(("groups", "dp"), "tensor"),
        P(("groups", "dp"), "tensor"),
    )
    out_specs = P(("groups", "dp"), "tensor")
    return jax.shard_map(body, mesh=mesh, in_specs=in_specs, out_specs=out_specs, check_vma=False)
```

profile of v0, /device:TPU:0, one launch (start us, length us, event | category | flops | bytes accessed | tf_op | source)
XLA Modules:
  0.0 441.2 jit_solution(8601654547606194414)
XLA Ops:
  6.5 0.7 fusion.8
  7.3 0.1 reduce_window_sum.11
  7.4 0.8 select_reduce_fusion
  8.2 0.7 fusion.11
  8.9 0.7 pad_add_fusion
  9.5 0.1 copy.15
  9.6 0.7 scatter_custom_fusion
  10.4 0.1 copy.16
  10.5 11.7 %all_to_all.10 = s32[4,24,2]{1,2,0:T(2,128)S(1)} all-to-all(s32[4,24,2]{1,2,0:T(2,128)S(1)} %copy.16), channel_id=1, replica_groups=mesh['groups'=2,'dp'=4,'tensor'=4] {'dp'}, dimensions={0} | all-to-all | bytes 1536 | tf_op jit(solution)/shard_map/all_to_all | solution.py:43
  22.2 0.1 reshape_squeeze.6
  22.3 0.1 iota_compare_fusion
  22.4 10.2 %gather_fusion = bf16[96,8,3,2048]{3,1,2,0:T(8,128)(2,1)} fusion(bf16[64,8,3,2048]{3,1,2,0:T(8,128)(2,1)} %param.7, s32[1024]{0:T(1024)S(1)} %pad_clamp_fusion.1), kind=kCustom, calls=%fused_computation | custom fusion | bytes 18874752 | tf_op jit(solution)/shard_map/jit(_take)/gather | solution.py:46
  32.6 8.5 %select_select_fusion = bf16[4,24,8,3,2048]{4,2,3,1,0:T(8,128)(2,1)} fusion(bf16[4,24,8,3,2048]{4,2,3,1,0:T(8,128)(2,1)} %bitcast.19, pred[4,24]{1,0:T(4,128)(4,1)S(1)} %compare_and_fusion, pred[4,24,8]{2,1,0:T(8,128)(4,1)S(1)} %iota_compare_fusion), kind=kLoop, calls=%fused_computation.8 | loop fusion | flops 9437184 | bytes 18875232 | tf_op jit(solution)/shard_map/jit(_where)/select_n | solution.py:47
  41.1 5.8 %all-to-all-start.1 = ((bf16[4,24,8,3,2048]{4,2,3,1,0:T(8,128)(2,1)}), bf16[4,24,8,3,2048]{4,2,3,1,0:T(8,128)(2,1)}, u32[]{:S(2)}, u32[]{:S(2)}) async-start(bf16[4,24,8,3,2048]{4,2,3,1,0:T(8,128)(2,1)} %select_select_fusion), calls=%async_computation.1 | async-start | bytes 18874368 | tf_op jit(solution)/shard_map/all_to_all | solution.py:49
  46.9 0.0 all-gather.3.cloned.1.call-start
  47.0 0.7 all-gather.3.cloned.1.call-update
  47.7 0.0 all-gather.5.cloned.1.call-start
  47.7 0.7 all-gather.5.cloned.1.call-update
  48.4 0.0 reduce-scatter.2.cloned.1.call-start
  48.5 202.9 %all-to-all-done.1 = bf16[4,24,8,3,2048]{4,2,3,1,0:T(8,128)(2,1)} async-done(((bf16[4,24,8,3,2048]{4,2,3,1,0:T(8,128)(2,1)}), bf16[4,24,8,3,2048]{4,2,3,1,0:T(8,128)(2,1)}, u32[]{:S(2)}, u32[]{:S(2)}) %all-to-all-start.1) | async-done | bytes 9437216 | tf_op jit(solution)/shard_map/all_to_all | solution.py:49
  251.3 0.0 copy-start
  251.3 7.3 %gather_fusion.1 = bf16[64,8,3,2048]{3,1,2,0:T(8,128)(2,1)} fusion(bf16[96,8,3,2048]{3,1,2,0:T(8,128)(2,1)} %bitcast.10, s32[1024]{0:T(1024)S(1)} %pad_clamp_fusion), kind=kCustom, calls=%fused_computation.1 | custom fusion | bytes 12583168 | tf_op jit(solution)/shard_map/gather | solution.py:50
  258.7 4.1 fusion
  262.8 0.1 copy.17
  262.9 10.1 %psum.7 = f32[64,8,3]{0,1,2:T(8,128)S(1)} all-reduce(f32[64,8,3]{0,1,2:T(8,128)S(1)} %copy.17), channel_id=1, replica_groups=mesh['groups'=2,'dp'=4,'tensor'=4] {'tensor'}, use_global_device_ids=true, to_apply=%region_4.5 | all-reduce | flops 1536 | bytes 12288 | tf_op jit(solution)/shard_map/psum | solution.py:53
  273.0 0.1 copy.18
  273.1 0.0 copy-done
  273.1 5.1 %fusion.2 = bf16[64,8,2048]{2,1,0:T(8,128)(2,1)S(1)} fusion(bf16[64,8,3,2048]{3,1,2,0:T(8,128)(2,1)} %gather_fusion.1, f32[3,2048]{1,0:T(4,128)S(1)} %copy-done, f32[64,8,3]{1,2,0:T(4,128)S(1)} %copy.18), kind=kLoop, calls=%fused_computation.7 | loop fusion | flops 11534336 | bytes 8419328 | tf_op jit(solution)/shard_map/reduce_sum | solution.py:55
  278.3 0.0 all-gather.3.cloned.1.call-done
  278.3 0.0 all-gather.5.cloned.1.call-done
  278.3 8.4 %convolution_convert_fusion = bf16[2048,2048]{1,0:T(8,128)(2,1)} fusion(bf16[512,1024]{1,0:T(8,128)(2,1)} %all-gather.5.cloned.1.call-done, bf16[512,1024]{1,0:T(8,128)(2,1)} %all-gather.3.cloned.1.call-done, bf16[64,8,2048]{2,1,0:T(8,128)(2,1)S(1)} %fusion.2), kind=kOutput, calls=%fused_computation.9 | convolution fusion | flops 4303355904 | bytes 12582912 | tf_op jit(solution)/shard_map/dot_general | solution.py:59
  286.7 0.0 reduce-scatter.2.cloned.1.call-update
  286.8 143.8 %reduce-scatter.2.cloned.1.call-done = bf16[512,2048]{1,0:T(8,128)(2,1)} async-done(((bf16[2048,2048]{1,0:T(8,128)(2,1)}), bf16[512,2048]{1,0:T(8,128)(2,1)}) %reduce-scatter.2.cloned.1.call-update) | async-done | bytes 2097168 | tf_op jit(solution)/shard_map/reduce_scatter | solution.py:58
  430.6 4.1 convert_element_type.24
  (6 shorter events, 0.1 us)
Async XLA Ops:
  41.1 210.2 %all-to-all-start.1 = ((bf16[4,24,8,3,2048]{4,2,3,1,0:T(8,128)(2,1)}), bf16[4,24,8,3,2048]{4,2,3,1,0:T(8,128)(2,1)}, u32[]{:S(2)}, u32[]{:S(2)}) async-start(bf16[4,24,8,3,2048]{4,2,3,1,0:T(8,128)(2,1)} %select_select_fusion), calls=%async_computation.1 | async-start | bytes 18874368 | tf_op jit(solution)/shard_map/all_to_all | solution.py:49
  46.9 231.3 %all-gather.3.cloned.1.call-start = ((), (), s32[]{:S(2)}) async-start(), calls=%async_computation.3 | async-start | bytes 1310720 | tf_op jit(solution)/shard_map/all_gather | solution.py:14
  47.7 230.6 %all-gather.5.cloned.1.call-start = ((), (), s32[]{:S(2)}) async-start(), calls=%async_computation.4 | async-start | bytes 1310720 | tf_op jit(solution)/shard_map/all_gather | solution.py:15
  48.4 382.1 %reduce-scatter.2.cloned.1.call-start = ((), (), s32[]{:S(2)}) async-start(), calls=%async_computation.5 | async-start | bytes 10485760 | tf_op jit(solution)/shard_map/reduce_scatter | solution.py:58
  251.3 21.8 %copy-start = (f32[3,2048]{1,0:T(4,128)S(1)}, f32[3,2048]{1,0:T(4,128)}, u32[]{:S(2)}) copy-start(f32[3,2048]{1,0:T(4,128)} %param.11) | copy-start | bytes 73732
Sparse Core Ops, SparseCore 0:
  49.3 18.2 all-gather.2
  69.2 16.8 all-gather.4
  286.9 143.6 reduce-scatter.1
where the time goes:
time: 442 us; the launch traced here: 441 us
  waiting for transfers between devices  348 us (79%)
  other arithmetic  25 us (6%)
  blocking collectives  21.8 us (5%)
  local copies, waits for them, and re-layouts  18.8 us (4%)
  between operations  13.2 us (3%)
  matrix products  8.41 us (2%)
  starting transfers between devices  5.92 us (1%)
    all_to_all x1, waiting for transfers between devices, body(): lax.all_to_all(shaped, 'dp', split_axis=0, concat_axis=0, tiled=True)  203 us
    reduce_scatter x1, waiting for transfers between devices, body(): lax.psum_scatter(lax.dot_general(cotangent, united, (((0,), (0,)), ((), (...  144 us
    all_to_all x1, blocking collectives, body(): lax.all_to_all(request, 'dp', split_axis=0, concat_axis=0, tiled=True)  11.7 us
    gather x1, local copies, waits for them, and re-layouts, body(): blocks = jnp.take(feature_cache, slots, axis=0)  10.2 us
    psum x1, blocking collectives, body(): summed = lax.psum(squares, 'tensor')  10.1 us
  transfers between devices with their start and end apart: 4, of which 2 were waited for; matrix products, arithmetic and copies ran while one was open for 4% of the time, Pallas kernels for 0%

commit v1 on v0

v1 whole, which is shorter than its diff:
```python
import jax
import jax.numpy as jnp
from jax import lax
from jax.sharding import PartitionSpec as P

EPSILON = 1e-06


def united_of(feature_cache, tap_gain, width):
    floats = feature_cache.astype(jnp.float32)
    squares = lax.psum(jnp.sum(floats * floats, axis=-1), "tensor")
    inverse_rms = lax.rsqrt(squares / width + EPSILON)
    return jnp.sum(floats * inverse_rms[..., None] * tap_gain, axis=2).astype(jnp.bfloat16)


def slot_matrix(owner_ids, slot_ids, live_tokens, owned, dtype):
    index = owner_ids[:, 0] * owned + slot_ids
    table = lax.all_gather(jnp.stack([index, live_tokens]), "dp", axis=1, tiled=True)
    slots = lax.axis_size("dp") * owned
    chosen = jnp.arange(slots, dtype=jnp.int32)[:, None] == table[0][None, :]
    return chosen.astype(dtype), table[1]


def body(feature_cache, owner_ids, slot_ids, live_tokens, tap_gain, key_cotangent, value_cotangent):
    owned, block_len, _, columns = feature_cache.shape
    width = columns * lax.axis_size("tensor")
    united = united_of(feature_cache, tap_gain, width).reshape(owned * block_len, columns)
    everywhere = lax.all_gather(united, "dp", axis=0, tiled=True)
    chosen, live = slot_matrix(owner_ids, slot_ids, live_tokens, owned, jnp.bfloat16)
    joined = jnp.concatenate(
        [
            lax.all_gather(key_cotangent, "tensor", axis=1, tiled=True),
            lax.all_gather(value_cotangent, "tensor", axis=1, tiled=True),
        ],
        axis=1,
    )
    mine = lax.all_to_all(joined, "dp", split_axis=1, concat_axis=0, tiled=True)
    rows = mine.shape[1]
    mine = mine.reshape(-1, block_len, rows)
    mask = jnp.arange(block_len, dtype=jnp.int32)[None, :] < live[:, None]
    mine = jnp.where(mask[:, :, None], mine, jnp.zeros_like(mine)).reshape(-1, block_len * rows)
    by_slot = lax.dot_general(
        chosen, mine, (((1,), (0,)), ((), ())), preferred_element_type=jnp.float32
    ).astype(jnp.bfloat16).reshape(-1, rows)
    return lax.dot_general(
        by_slot, everywhere, (((0,), (0,)), ((), ())), preferred_element_type=jnp.float32
    )


def solution(mesh):
    in_specs = (
        P(("groups", "dp"), None, None, "tensor"),
        P(("groups", "dp"), None),
        P(("groups", "dp")),
        P(("groups", "dp")),
        P(None, "tensor"),
        P(("groups", "dp"), "tensor"),
        P(("groups", "dp"), "tensor"),
    )
    out_specs = P(("groups", "dp"), "tensor")
    return jax.shard_map(body, mesh=mesh, in_specs=in_specs, out_specs=out_specs, check_vma=False)
```

time: 442 us -> 255 us (0.58)
  waiting for transfers between devices: 348 us -> 118 us
  blocking collectives: 21.8 us -> 84.5 us
  other arithmetic: 25 us -> 12.9 us
  local copies, waits for them, and re-layouts: 18.8 us -> 8.19 us
  matrix products: 8.41 us -> 13.1 us
    all_to_all x1, waiting for transfers between devices: 203 us -> 32.2 us  [body(): mine = lax.all_to_all(joined, 'dp', split_axis=1, concat_axis=0, tiled=True)]
    reduce_scatter x1 -> x0, waiting for transfers between devices: 144 us -> none  [body(): lax.psum_scatter(lax.dot_general(cotangent, united, (((0,), (0,)), ((), (...]
    all_gather x2 -> x3, waiting for transfers between devices: 0.04 us -> 84.8 us  [the longest x1 70.2 us: body(): everywhere = lax.all_gather(united, 'dp', axis=0, tiled=True)]
    all_gather x0 -> x1, blocking collectives: none -> 71.3 us  [slot_matrix(): lax.all_gather(jnp.stack([index, live_tokens]), 'dp', axis=1, tiled=True)]
    gather x2 -> x0, local copies, waits for them, and re-layouts: 17.6 us -> none  [the longest x1 10.2 us: body(): blocks = jnp.take(feature_cache, slots, axis=0)]
    all_to_all x1 -> x0, blocking collectives: 11.7 us -> none  [body(): lax.all_to_all(request, 'dp', split_axis=0, concat_axis=0, tiled=True)]
    select_n x3 -> x0, other arithmetic: 9.19 us -> none  [the longest x1 8.51 us: body(): jnp.where(live_mask[:, :, None, None], blocks, jnp.zeros_like(blocks))]
    reshape x1 -> x2, local copies, waits for them, and re-layouts: 0.09 us -> 5.2 us  [the longest x1 2.87 us: body(): by_slot = lax.dot_general(chosen, mine, (((1,), (0,)), ((), ())), preferr...]
  transfers between devices with their start and end apart: 4 -> 4, of which waited for: 2 -> 3; matrix products, arithmetic and copies ran while one was open for 4% -> 10% of each run, Pallas kernels for 0% -> 0%
where the time goes in v1:
time: 255 us
  waiting for transfers between devices  118 us (46%)
  blocking collectives  84.5 us (33%)
  between operations  13.2 us (5%)
  matrix products  13.1 us (5%)
  other arithmetic  12.9 us (5%)
  local copies, waits for them, and re-layouts  8.19 us (3%)
  starting transfers between devices  4.68 us (2%)
    all_gather x1, blocking collectives, slot_matrix(): lax.all_gather(jnp.stack([index, live_tokens]), 'dp', axis=1, tiled=True)  71.3 us
    all_gather x1, waiting for transfers between devices, body(): everywhere = lax.all_gather(united, 'dp', axis=0, tiled=True)  70.2 us
    all_to_all x1, waiting for transfers between devices, body(): mine = lax.all_to_all(joined, 'dp', split_axis=1, concat_axis=0, tiled=True)  32.2 us
    all_gather x1, waiting for transfers between devices, body(): lax.all_gather(value_cotangent, 'tensor', axis=1, tiled=True)  14.6 us
    psum x1, blocking collectives, united_of(): squares = lax.psum(jnp.sum(floats * floats, axis=-1), 'tensor')  13.1 us
    dot_general x1, matrix products, body(): lax.dot_general(by_slot, everywhere, (((0,), (0,)), ((), ())), preferred_...  9.44 us
    reduce_sum x1, other arithmetic, united_of(): jnp.sum(floats * inverse_rms[..., None] * tap_gain, axis=2)  6.9 us
  transfers between devices with their start and end apart: 4, of which 3 were waited for; matrix products, arithmetic and copies ran while one was open for 10% of the time, Pallas kernels for 0%

profile of v1, /device:TPU:0, one launch (start us, length us, event | category | flops | bytes accessed | tf_op | source)
XLA Modules:
  0.0 255.0 jit_solution(5300680193255701381)
XLA Ops:
  6.5 0.0 copy-start
  6.5 0.0 all-gather.5.cloned.1.call-start
  6.5 0.7 all-gather.5.cloned.1.call-update
  7.3 0.0 all-gather.7.cloned.1.call-start
  7.3 0.7 all-gather.7.cloned.1.call-update
  8.0 0.0 all-gather.9.cloned.1.call-start
  8.1 4.1 %fusion = f32[64,8,3]{1,2,0:T(4,128)S(1)} fusion(bf16[64,8,3,2048]{3,1,2,0:T(8,128)(2,1)} %param.7), kind=kLoop, calls=%fused_computation.2 | loop fusion | flops 9435648 | bytes 6297600 | tf_op jit(solution)/shard_map/reduce_sum | solution.py:11
  12.2 0.1 copy.17
  12.3 13.1 %psum.7 = f32[64,8,3]{0,1,2:T(8,128)S(1)} all-reduce(f32[64,8,3]{0,1,2:T(8,128)S(1)} %copy.17), channel_id=1, replica_groups=mesh['groups'=2,'dp'=4,'tensor'=4] {'tensor'}, use_global_device_ids=true, to_apply=%region_1.0 | all-reduce | flops 1536 | bytes 12288 | tf_op jit(solution)/shard_map/psum | solution.py:11
  25.4 0.1 copy.18
  25.5 0.0 copy-done
  25.5 6.9 %fusion.2 = bf16[64,8,2048]{2,1,0:T(8,128)(2,1)} fusion(bf16[64,8,3,2048]{3,1,2,0:T(8,128)(2,1)} %param.7, f32[3,2048]{1,0:T(4,128)S(1)} %copy-done, f32[64,8,3]{1,2,0:T(4,128)S(1)} %copy.18), kind=kLoop, calls=%fused_computation.4 | loop fusion | flops 11534336 | bytes 8419328 | tf_op jit(solution)/shard_map/reduce_sum | solution.py:13
  32.4 0.0 all-gather.9.cloned.1.call-update
  32.5 0.0 all-gather.5.cloned.1.call-done
  32.5 14.6 %all-gather.7.cloned.1.call-done = bf16[512,1024]{1,0:T(8,128)(2,1)} async-done(((bf16[512,256]{1,0:T(8,128)(2,1)}), bf16[512,1024]{1,0:T(8,128)(2,1)}) %all-gather.7.cloned.1.call-update) | async-done | bytes 1048592 | tf_op jit(solution)/shard_map/all_gather | solution.py:33
  47.0 1.7 pad_maximum_fusion
  48.8 0.0 copy-start.2
  48.8 0.0 copy-start.3
  48.8 0.0 copy-start.1
  48.8 1.5 copy.22
  50.3 4.6 %all-to-all-start = ((bf16[512,4,512]{2,0,1:T(8,128)(2,1)}), bf16[512,4,512]{2,0,1:T(8,128)(2,1)S(1)}, u32[]{:S(2)}, u32[]{:S(2)}) async-start(bf16[512,4,512]{2,0,1:T(8,128)(2,1)} %bitcast.29), calls=%async_computation | async-start | bytes 4194304 | tf_op jit(solution)/shard_map/all_to_all | solution.py:37
  54.9 0.0 copy-done.2
  54.9 0.0 copy-done.3
  54.9 0.0 copy-done.1
  55.0 71.3 %all-gather = s32[4,64,2]{1,2,0:T(2,128)S(1)} all-gather(s32[1,64,2]{1,2,0:T(2,128)S(1)} %add_bitcast_fusion), channel_id=1, replica_groups=mesh['groups'=2,'dp'=4,'tensor'=4] {'dp'}, dimensions={0}, use_global_device_ids=true | all-gather | bytes 2560 | tf_op jit(solution)/shard_map/all_gather | solution.py:18
  126.3 0.1 reshape.47
  126.4 0.1 iota_compare_fusion.2
  126.5 0.5 broadcast_in_dim.18
  126.9 0.8 copy.20
  127.7 32.2 %all-to-all-done = bf16[512,4,512]{2,0,1:T(8,128)(2,1)S(1)} async-done(((bf16[512,4,512]{2,0,1:T(8,128)(2,1)}), bf16[512,4,512]{2,0,1:T(8,128)(2,1)S(1)}, u32[]{:S(2)}, u32[]{:S(2)}) %all-to-all-start) | async-done | bytes 2097184 | tf_op jit(solution)/shard_map/all_to_all | solution.py:37
  159.9 2.3 reshape.44
  162.3 3.7 %convolution_convert_fusion = bf16[256,4096]{1,0:T(8,128)(2,1)} fusion(pred[256,4096]{1,0:T(8,128)(4,1)S(1)} %bitcast.33, bf16[256,4096]{1,0:T(8,128)(2,1)} %reshape.44, s32[256]{0:T(256)S(1)} %bitcast.36), kind=kOutput, calls=%fused_computation.5 | convolution fusion | flops 539033600 | bytes 5243904 | tf_op jit(solution)/shard_map/dot_general | solution.py:42
  165.9 2.9 %reshape.45 = bf16[2048,512]{1,0:T(8,128)(2,1)S(1)} reshape(bf16[256,4096]{1,0:T(8,128)(2,1)} %convolution_convert_fusion) | data formatting | bytes 4194304 | tf_op jit(solution)/shard_map/reshape | solution.py:44
  168.8 70.2 %all-gather.9.cloned.1.call-done = bf16[2048,2048]{1,0:T(8,128)(2,1)} async-done(((bf16[512,2048]{1,0:T(8,128)(2,1)}), bf16[2048,2048]{1,0:T(8,128)(2,1)}) %all-gather.9.cloned.1.call-update) | async-done | bytes 8388624 | tf_op jit(solution)/shard_map/all_gather | solution.py:28
  239.0 9.4 %fusion.9 = f32[512,2048]{1,0:T(8,128)} fusion(bf16[2048,512]{1,0:T(8,128)(2,1)S(1)} %reshape.45, bf16[2048,2048]{1,0:T(8,128)(2,1)} %all-gather.9.cloned.1.call-done), kind=kOutput, calls=%fused_computation.20 | convolution fusion | flops 4294967296 | bytes 14680064 | tf_op jit(solution)/shard_map/dot_general | solution.py:45
  (5 shorter events, 0.0 us)
Async XLA Ops:
  6.5 19.0 %copy-start = (f32[3,2048]{1,0:T(4,128)S(1)}, f32[3,2048]{1,0:T(4,128)}, u32[]{:S(2)}) copy-start(f32[3,2048]{1,0:T(4,128)} %param.11) | copy-start | bytes 73732
  6.5 25.9 %all-gather.5.cloned.1.call-start = ((), (), s32[]{:S(2)}) async-start(), calls=%async_computation.1 | async-start | bytes 1310720 | tf_op jit(solution)/shard_map/all_gather | solution.py:32
  7.3 39.8 %all-gather.7.cloned.1.call-start = ((), (), s32[]{:S(2)}) async-start(), calls=%async_computation.2 | async-start | bytes 1310720 | tf_op jit(solution)/shard_map/all_gather | solution.py:33
  8.0 231.0 %all-gather.9.cloned.1.call-start = ((), (), s32[]{:S(2)}) async-start(), calls=%async_computation.3 | async-start | bytes 10485760 | tf_op jit(solution)/shard_map/all_gather | solution.py:28
  48.8 6.1 %copy-start.2 = (s32[64]{0:T(128)S(1)}, s32[64]{0:T(128)}, u32[]{:S(2)}) copy-start(s32[64]{0:T(128)} %param.9) | copy-start | bytes 772
  48.8 6.1 %copy-start.3 = (s32[64,1]{0,1:T(1,128)S(1)}, s32[64,1]{0,1:T(1,128)}, u32[]{:S(2)}) copy-start(s32[64,1]{0,1:T(1,128)} %param.8) | copy-start | bytes 772
  48.8 6.1 %copy-start.1 = (s32[64]{0:T(128)S(1)}, s32[64]{0:T(128)}, u32[]{:S(2)}) copy-start(s32[64]{0:T(128)} %param.10) | copy-start | bytes 772
  50.3 109.6 %all-to-all-start = ((bf16[512,4,512]{2,0,1:T(8,128)(2,1)}), bf16[512,4,512]{2,0,1:T(8,128)(2,1)S(1)}, u32[]{:S(2)}, u32[]{:S(2)}) async-start(bf16[512,4,512]{2,0,1:T(8,128)(2,1)} %bitcast.29), calls=%async_computation | async-start | bytes 4194304 | tf_op jit(solution)/shard_map/all_to_all | solution.py:37
Sparse Core Ops, SparseCore 0:
  8.9 19.6 all-gather.4
  30.2 16.8 all-gather.6
  48.6 190.3 all-gather.8

commit v2 on v1

--- a/solution.py
+++ b/solution.py
@@ -1,6 +1,8 @@
 import jax
 import jax.numpy as jnp
 from jax import lax
+from jax.experimental import pallas as pl
+from jax.experimental.pallas import tpu as pltpu
 from jax.sharding import PartitionSpec as P
 
 EPSILON = 1e-06
@@ -21,7 +23,7 @@
     return chosen.astype(dtype), table[1]
 
 
-def body(feature_cache, owner_ids, slot_ids, live_tokens, tap_gain, key_cotangent, value_cotangent):
+def general_body(feature_cache, owner_ids, slot_ids, live_tokens, tap_gain, key_cotangent, value_cotangent):
     owned, block_len, _, columns = feature_cache.shape
     width = columns * lax.axis_size("tensor")
     united = united_of(feature_cache, tap_gain, width).reshape(owned * block_len, columns)
@@ -47,6 +49,200 @@
     )
 
 
+MESH = pl.DeviceIdType.MESH
+CHUNK = 256
+
+
+def line_kernel(
+    u_in, idx_in, mine_in, near_in, mid_in, far_in, out,
+    uall, cbuf, select, st, gbuf, stage, outv, idxv,
+    usend, urecv, csend, crecv, gsend, grecv, osem, lsem, isend, irecv,
+):
+    z, c = lax.axis_index("dp"), lax.axis_index("tensor")
+    tok, columns = u_in.shape
+    share = mine_in.shape[1]
+    chunks = columns // CHUNK
+    sibling, across = c + 1 - 2 * lax.rem(c, 2), lax.rem(c + 2, 4)
+    across_sibling = lax.rem(sibling + 2, 4)
+    is_hub = (z == 1) | (z == 2)
+
+    def remote(src, dst, ss, rs, dz, dc):
+        return pltpu.make_async_remote_copy(
+            src_ref=src, dst_ref=dst, send_sem=ss, recv_sem=rs,
+            device_id={"dp": dz, "tensor": dc}, device_id_type=MESH,
+        )
+
+    def cols(j):
+        return pl.ds(pl.multiple_of(j * CHUNK, CHUNK), CHUNK)
+
+    own_u = pltpu.make_async_copy(u_in, uall.at[z], lsem.at[0])
+    own_idx = pltpu.make_async_copy(idx_in, idxv.at[z], lsem.at[1])
+    own_u.start()
+    own_idx.start()
+
+    barrier = pltpu.get_barrier_semaphore()
+    for step in range(1, 4):
+        pl.semaphore_signal(
+            barrier, inc=1, device_id={"dp": lax.rem(z + step, 4), "tensor": c}, device_id_type=MESH
+        )
+    for peer in (sibling, across):
+        pl.semaphore_signal(barrier, inc=1, device_id={"dp": z, "tensor": peer}, device_id_type=MESH)
+    pl.semaphore_wait(barrier, 5)
+    own_u.wait()
+    own_idx.wait()
+
+    def u_copy(owner, j, sem, dz):
+        return remote(uall.at[owner, :, cols(j)], uall.at[owner, :, cols(j)], sem, urecv.at[owner, j], dz, c)
+
+    def idx_copy(owner, sem, dz):
+        return remote(idxv.at[owner], idxv.at[owner], sem, irecv.at[owner], dz, c)
+
+    def out_copy(j):
+        return pltpu.make_async_copy(outv.at[:, cols(j)], out.at[:, cols(j)], osem.at[j])
+
+    def g_copy(j, dz):
+        return remote(stage.at[:, cols(j)], gbuf.at[:, cols(j)], gsend.at[j], grecv.at[j], dz, c)
+
+    @pl.when(jnp.logical_not(is_hub))
+    def _():
+        hub = 1 + z // 3
+        for n, dz in enumerate((hub, 3 - hub)):
+            idx_copy(z, isend.at[n], dz).start()
+        for j in range(chunks):
+            u_copy(z, j, usend.at[0, j], hub).start()
+        for n, dz in enumerate((hub, 3 - hub)):
+            idx_copy(z, isend.at[n], dz).wait_send()
+
+        def take(j, carry):
+            g_copy(j, hub).wait_recv()
+            outv[:, cols(j)] = gbuf[:, cols(j)].astype(jnp.float32)
+            out_copy(j).start()
+            return carry
+
+        lax.fori_loop(0, chunks, take, 0)
+        for j in range(chunks):
+            u_copy(z, j, usend.at[0, j], hub).wait_send()
+            out_copy(j).wait()
+
+    @pl.when(is_hub)
+    def _():
+        leaf, other = 3 * (z - 1), 3 - z
+        far_leaf = 3 - leaf
+        idx_copy(z, isend.at[0], other).start()
+        places = (z, leaf, other, far_leaf)
+        loads = []
+        for n, (ref, place) in enumerate(zip((mine_in, near_in, mid_in, far_in), places)):
+            loads.append(pltpu.make_async_copy(ref, cbuf.at[c, pl.ds(pl.multiple_of(place * tok, tok), tok)], lsem.at[2 + n]))
+            loads[n].start()
+
+        def c_copy(kind, n, who, dc):
+            part = cbuf.at[who, pl.ds(pl.multiple_of(places[n] * tok, tok), tok)]
+            return remote(part, part, csend.at[kind, n], crecv.at[kind, n], z, dc)
+
+        for n in range(4):
+            loads[n].wait()
+            c_copy(0, n, c, across).start()
+            c_copy(1, n, c, sibling).start()
+        for j in range(chunks):
+            u_copy(z, j, usend.at[0, j], other).start()
+        for place in (leaf, other, far_leaf):
+            idx_copy(place, isend.at[0], other).wait_recv()
+        idx_copy(z, isend.at[0], other).wait_send()
+
+        def fill(s, carry):
+            rows = lax.broadcasted_iota(jnp.int32, (tok, tok), 0) + s * tok
+            for k in range(4):
+                hit = idxv[k][0:1, :] == rows
+                select[pl.ds(pl.multiple_of(s * tok, tok), tok), k * tok:(k + 1) * tok] = jnp.where(
+                    hit, 1.0, 0.0
+                ).astype(jnp.bfloat16)
+            return carry
+
+        lax.fori_loop(0, 4, fill, 0)
+        for n in range(4):
+            c_copy(0, n, across, across).wait_recv()
+            c_copy(2, n, across, sibling).start()
+
+        def hand_on(j):
+            u_copy(leaf, j, usend.at[1, j], other).wait_recv()
+            u_copy(leaf, j, usend.at[1, j], other).start()
+
+        for n in range(4):
+            c_copy(1, n, sibling, sibling).wait_recv()
+        for n in range(4):
+            c_copy(2, n, across_sibling, sibling).wait_recv()
+
+        def by_slot(k, carry):
+            st[k // 2, pl.ds(pl.multiple_of(lax.rem(k, 2) * share, share), share), :] = lax.dot_general(
+                cbuf[k], select[...], (((0,), (1,)), ((), ())), preferred_element_type=jnp.float32
+            ).astype(jnp.bfloat16)
+            for step in range(chunks // 4):
+                hand_on(k * (chunks // 4) + step)
+            return carry
+
+        lax.fori_loop(0, 4, by_slot, 0)
+
+        def finish(j, carry):
+            u_copy(other, j, usend.at[0, j], other).wait_recv()
+            u_copy(far_leaf, j, usend.at[0, j], other).wait_recv()
+            part = uall[:, :, cols(j)].reshape(4 * tok, CHUNK)
+            stage[:, cols(j)] = jnp.dot(st[z - 1], part, preferred_element_type=jnp.float32).astype(jnp.bfloat16)
+            g_copy(j, leaf).start()
+            outv[:, cols(j)] = jnp.dot(st[2 - z], part, preferred_element_type=jnp.float32)
+            out_copy(j).start()
+            return carry
+
+        lax.fori_loop(0, chunks, finish, 0)
+        for n in range(4):
+            c_copy(0, n, c, across).wait_send()
+            c_copy(1, n, c, sibling).wait_send()
+            c_copy(2, n, across, sibling).wait_send()
+        for j in range(chunks):
+            u_copy(z, j, usend.at[0, j], other).wait_send()
+            u_copy(leaf, j, usend.at[1, j], other).wait_send()
+            g_copy(j, leaf).wait_send()
+            out_copy(j).wait()
+
+
+def line_body(feature_cache, owner_ids, slot_ids, live_tokens, tap_gain, key_cotangent, value_cotangent):
+    owned, block_len, _, columns = feature_cache.shape
+    tok, share = key_cotangent.shape
+    chunks = columns // CHUNK
+    z = lax.axis_index("dp")
+    near = lax.ppermute(jnp.where((z == 0), key_cotangent, value_cotangent), "dp", [(0, 1), (3, 2)])
+    mid = lax.ppermute(jnp.where((z == 2), key_cotangent, value_cotangent), "dp", [(1, 2), (2, 1)])
+    far = lax.ppermute(jnp.where((z == 3), key_cotangent, value_cotangent), "dp", [(0, 2), (3, 1)])
+    mine = jnp.where(z == 1, key_cotangent, value_cotangent)
+    offsets = jnp.arange(block_len, dtype=jnp.int32)
+    first = (owner_ids[:, 0] * owned + slot_ids) * block_len
+    index = jnp.where(offsets[None, :] < live_tokens[:, None], first[:, None] + offsets[None, :], -1)
+    index = jnp.broadcast_to(index.reshape(1, tok), (8, tok))
+    united = united_of(feature_cache, tap_gain, columns * lax.axis_size("tensor")).reshape(tok, columns)
+    anywhere = pl.BlockSpec(memory_space=pl.ANY)
+    dma = pltpu.SemaphoreType.DMA
+    return pl.pallas_call(
+        line_kernel,
+        out_shape=jax.ShapeDtypeStruct((tok, columns), jnp.float32),
+        in_specs=[anywhere] * 6,
+        out_specs=anywhere,
+        scratch_shapes=[
+            pltpu.VMEM((4, tok, columns), jnp.bfloat16),
+            pltpu.VMEM((4, 4 * tok, share), jnp.bfloat16),
+            pltpu.VMEM((4 * tok, 4 * tok), jnp.bfloat16),
+            pltpu.VMEM((2, 2 * share, 4 * tok), jnp.bfloat16),
+            pltpu.VMEM((tok, columns), jnp.bfloat16),
+            pltpu.VMEM((tok, columns), jnp.bfloat16),
+            pltpu.VMEM((tok, columns), jnp.float32),
+            pltpu.VMEM((4, 8, tok), jnp.int32),
+            dma((2, chunks)), dma((4, chunks)), dma((3, 4)), dma((3, 4)),
+            dma((chunks,)), dma((chunks,)), dma((chunks,)), dma((6,)), dma((2,)), dma((4,)),
+        ],
+        compiler_params=pltpu.CompilerParams(
+            collective_id=0, has_side_effects=True, vmem_limit_bytes=56 * 1024 * 1024
+        ),
+    )(united, index, mine, near, mid, far)
+
+
 def solution(mesh):
     in_specs = (
         P(("groups", "dp"), None, None, "tensor"),
@@ -57,5 +253,6 @@
         P(("groups", "dp"), "tensor"),
         P(("groups", "dp"), "tensor"),
     )
+    body = line_body if mesh.shape["dp"] == 4 and mesh.shape["tensor"] == 4 else general_body
     out_specs = P(("groups", "dp"), "tensor")
     return jax.shard_map(body, mesh=mesh, in_specs=in_specs, out_specs=out_specs, check_vma=False)

time: 255 us -> 142 us (0.56)
  waiting for transfers between devices: 118 us -> 0.01 us
  Pallas kernels: 0 us -> 104 us
  blocking collectives: 84.5 us -> 10.6 us
  matrix products: 13.1 us -> 0 us
  between operations: 13.2 us -> 0.14 us
  starting transfers between devices: 4.68 us -> 8.06 us
    pallas_call x0 -> x1, Pallas kernels: none -> 104 us  [line_body(): pl.pallas_call(line_kernel, out_shape=jax.ShapeDtypeStruct((tok, columns)...]
    all_gather x3 -> x0, waiting for transfers between devices: 84.8 us -> none  [the longest x1 70.2 us: body(): everywhere = lax.all_gather(united, 'dp', axis=0, tiled=True)]
    all_gather x1 -> x0, blocking collectives: 71.3 us -> none  [slot_matrix(): lax.all_gather(jnp.stack([index, live_tokens]), 'dp', axis=1, tiled=True)]
    all_to_all x1 -> x0, waiting for transfers between devices: 32.2 us -> none  [body(): mine = lax.all_to_all(joined, 'dp', split_axis=1, concat_axis=0, tiled=True)]
    dot_general x2 -> x0, matrix products: 13.1 us -> none  [the longest x1 9.44 us: body(): lax.dot_general(by_slot, everywhere, (((0,), (0,)), ((), ())), preferred_...]
    ppermute x0 -> x3, starting transfers between devices: none -> 8.06 us  [the longest x1 5.94 us: line_body(): lax.ppermute(jnp.where(z == 3, key_cotangent, value_cotangent), 'dp', [(0...]
    reshape x2 -> x0, local copies, waits for them, and re-layouts: 5.2 us -> none  [the longest x1 2.87 us: body(): by_slot = lax.dot_general(chosen, mine, (((1,), (0,)), ((), ())), preferr...]
    all_to_all x1 -> x0, starting transfers between devices: 4.6 us -> none  [body(): mine = lax.all_to_all(joined, 'dp', split_axis=1, concat_axis=0, tiled=True)]
  transfers between devices with their start and end apart: 4 -> 3, of which waited for: 3 -> 0; matrix products, arithmetic and copies ran while one was open for 10% -> 8% of each run, Pallas kernels for 0% -> 0%
where the time goes in v2:
time: 142 us; the launch traced here: 141 us
  Pallas kernels  104 us (73%)
  other arithmetic  12.8 us (9%)
  blocking collectives  10.6 us (7%)
  starting transfers between devices  8.06 us (6%)
  local copies, waits for them, and re-layouts  5.86 us (4%)
    pallas_call x1, Pallas kernels, line_body(): pl.pallas_call(line_kernel, out_shape=jax.ShapeDtypeStruct((tok, columns)...  104 us
    psum x1, blocking collectives, united_of(): squares = lax.psum(jnp.sum(floats * floats, axis=-1), 'tensor')  10.6 us
    reduce_sum x1, other arithmetic, united_of(): jnp.sum(floats * inverse_rms[..., None] * tap_gain, axis=2)  6.82 us
    ppermute x1, starting transfers between devices, line_body(): lax.ppermute(jnp.where(z == 3, key_cotangent, value_cotangent), 'dp', [(0...  5.94 us
    unnamed x15, local copies, waits for them, and re-layouts  4.88 us
    reduce_sum x1, other arithmetic, united_of(): squares = lax.psum(jnp.sum(floats * floats, axis=-1), 'tensor')  4.12 us
  transfers between devices with their start and end apart: 3, of which 0 were waited for; matrix products, arithmetic and copies ran while one was open for 8% of the time, Pallas kernels for 0%

profile of v2, /device:TPU:0, one launch (start us, length us, event | category | flops | bytes accessed | tf_op | source)
XLA Modules:
  0.0 141.3 jit_solution(16768974942672879472)
XLA Ops:
  0.0 0.0 copy-start.3
  0.0 1.8 %broadcast_select_fusion = (bf16[512,256]{1,0:T(8,128)(2,1)S(1)}, bf16[512,256]{1,0:T(8,128)(2,1)S(1)}, bf16[512,256]{1,0:T(8,128)(2,1)}, bf16[512,256]{1,0:T(8,128)(2,1)S(1)}) fusion(bf16[512,256]{1,0:T(8,128)(2,1)} %param.12, bf16[512,256]{1,0:T(8,128)(2,1)} %param.13, pred[]{:T(512)S(6)} %eq.15, pred[]{:T(512)S(6)} %eq.13, pred[]{:T(512)S(6)} %eq.12, ...), kind=kLoop, calls=%fused_computation.6 | loop fusion | flops 524288 | bytes 1572868 | tf_op jit(solution)/shard_map/jit(_where)/select_n | solution.py:214
  1.8 5.9 %collective-permute-start.2 = (bf16[512,256]{1,0:T(8,128)(2,1)S(1)}, bf16[512,256]{1,0:T(8,128)(2,1)S(1)}, u32[]{:S(2)}, u32[]{:S(2)}) collective-permute-start(bf16[512,256]{1,0:T(8,128)(2,1)S(1)} %get-tuple-element.5), channel_id=1, source_target_pairs={{0,8},{12,4},{1,9},{13,5},{2,10},{14,6},{3,11},{15,7},{16,24},{28,... | collective-permute-start | bytes 786440 | tf_op jit(solution)/shard_map/ppermute | solution.py:214
  7.8 1.3 collective-permute-start
  9.1 0.0 copy-start.5
  9.1 0.0 copy-start.6
  9.1 0.0 copy-start.4
  9.1 0.8 collective-permute-start.1
  9.9 4.1 %fusion = f32[64,8,3]{1,2,0:T(4,128)S(1)} fusion(bf16[64,8,3,2048]{3,1,2,0:T(8,128)(2,1)} %param.7), kind=kLoop, calls=%fused_computation.2 | loop fusion | flops 9435648 | bytes 6297600 | tf_op jit(solution)/shard_map/reduce_sum | solution.py:13
  14.0 0.1 copy.9
  14.1 10.6 %psum.7 = f32[64,8,3]{0,1,2:T(8,128)S(1)} all-reduce(f32[64,8,3]{0,1,2:T(8,128)S(1)} %copy.9), channel_id=1, replica_groups=mesh['groups'=2,'dp'=4,'tensor'=4] {'tensor'}, use_global_device_ids=true, to_apply=%region_1.2 | all-reduce | flops 1536 | bytes 12288 | tf_op jit(solution)/shard_map/psum | solution.py:13
  24.7 0.1 copy.10
  24.8 0.0 copy-done.3
  24.8 6.8 %fusion.2 = bf16[64,8,2048]{2,1,0:T(8,128)(2,1)} fusion(bf16[64,8,3,2048]{3,1,2,0:T(8,128)(2,1)} %param.7, f32[3,2048]{1,0:T(4,128)S(1)} %copy-done.3, f32[64,8,3]{1,2,0:T(4,128)S(1)} %copy.10), kind=kLoop, calls=%fused_computation.4 | loop fusion | flops 11534336 | bytes 8419328 | tf_op jit(solution)/shard_map/reduce_sum | solution.py:15
  31.7 0.0 copy-done.5
  31.7 0.0 copy-done.6
  31.7 0.0 copy-done.4
  31.7 0.1 add_select_fusion
  31.8 0.1 select_n.38
  31.9 0.0 collective-permute-done.2.far_in
  31.9 0.0 copy-start
  31.9 0.0 collective-permute-done.near_in
  31.9 0.0 copy-start.1
  31.9 0.0 collective-permute-done.1.mid_in
  31.9 0.0 copy-start.2
  31.9 0.7 broadcast_in_dim.7.idx_in
  32.6 0.0 copy-done
  32.6 0.1 copy-done.1
  32.7 0.1 copy-done.2
  32.8 103.8 %shard_map.73 = f32[512,2048]{1,0:T(8,128)} custom-call(bf16[512,2048]{1,0:T(8,128)(2,1)} %bitcast.7, s32[8,512]{1,0:T(8,128)} %broadcast_in_dim.7.idx_in, bf16[512,256]{1,0:T(8,128)(2,1)} %get-tuple-element.7.mine_in, bf16[512,256]{1,0:T(8,128)(2,1)} %copy-done.1, bf16[512,256]{1,0:T(8,128)(2,1)} %copy-done.2, bf16[512,256]{1,0:T(8,128)(2,1)} %copy-done), custom_call_target="tpu_custom_call" | custom-call | tf_op jit(solution)/shard_map/pallas_call | solution.py:223
  136.6 4.7 %copy.12 = f32[512,2048]{1,0:T(8,128)} copy(f32[512,2048]{1,0:T(8,128)} %shard_map.73) | data formatting | bytes 8388608
  (2 shorter events, 0.0 us)
Async XLA Ops:
  0.0 24.8 %copy-start.3 = (f32[3,2048]{1,0:T(4,128)S(1)}, f32[3,2048]{1,0:T(4,128)}, u32[]{:S(2)}) copy-start(f32[3,2048]{1,0:T(4,128)} %param.11) | copy-start | bytes 73732
  1.8 30.1 %collective-permute-start.2 = (bf16[512,256]{1,0:T(8,128)(2,1)S(1)}, bf16[512,256]{1,0:T(8,128)(2,1)S(1)}, u32[]{:S(2)}, u32[]{:S(2)}) collective-permute-start(bf16[512,256]{1,0:T(8,128)(2,1)S(1)} %get-tuple-element.5), channel_id=1, source_target_pairs={{0,8},{12,4},{1,9},{13,5},{2,10},{14,6},{3,11},{15,7},{16,24},{28,... | collective-permute-start | bytes 786440 | tf_op jit(solution)/shard_map/ppermute | solution.py:214
  7.8 24.1 %collective-permute-start = (bf16[512,256]{1,0:T(8,128)(2,1)S(1)}, bf16[512,256]{1,0:T(8,128)(2,1)S(1)}, u32[]{:S(2)}, u32[]{:S(2)}) collective-permute-start(bf16[512,256]{1,0:T(8,128)(2,1)S(1)} %get-tuple-element.6), channel_id=1, source_target_pairs={{0,4},{12,8},{1,5},{13,9},{2,6},{14,10},{3,7},{15,11},{16,20},{28,... | collective-permute-start | bytes 786440 | tf_op jit(solution)/shard_map/ppermute | solution.py:212
  9.1 22.6 %copy-start.5 = (s32[64]{0:T(128)S(1)}, s32[64]{0:T(128)}, u32[]{:S(2)}) copy-start(s32[64]{0:T(128)} %param.9) | copy-start | bytes 772
  9.1 22.6 %copy-start.6 = (s32[64,1]{0,1:T(1,128)S(1)}, s32[64,1]{0,1:T(1,128)}, u32[]{:S(2)}) copy-start(s32[64,1]{0,1:T(1,128)} %param.8) | copy-start | bytes 772
  9.1 22.6 %copy-start.4 = (s32[64]{0:T(128)S(1)}, s32[64]{0:T(128)}, u32[]{:S(2)}) copy-start(s32[64]{0:T(128)} %param.10) | copy-start | bytes 772
  9.1 22.8 %collective-permute-start.1 = (bf16[512,256]{1,0:T(8,128)(2,1)S(1)}, bf16[512,256]{1,0:T(8,128)(2,1)S(1)}, u32[]{:S(2)}, u32[]{:S(2)}) collective-permute-start(bf16[512,256]{1,0:T(8,128)(2,1)S(1)} %get-tuple-element.8), channel_id=1, source_target_pairs={{4,8},{8,4},{5,9},{9,5},{6,10},{10,6},{7,11},{11,7},{20,24},{24,20... | collective-permute-start | bytes 786440 | tf_op jit(solution)/shard_map/ppermute | solution.py:213
  31.9 0.8 copy-start
  31.9 0.8 copy-start.1
  31.9 0.9 copy-start.2

commit v3 on v2

v3 whole, which is shorter than its diff:
```python
import jax
import jax.numpy as jnp
from jax import lax
from jax.experimental import pallas as pl
from jax.experimental.pallas import tpu as pltpu
from jax.sharding import PartitionSpec as P

EPSILON = 1e-06


def united_of(feature_cache, tap_gain, width):
    floats = feature_cache.astype(jnp.float32)
    squares = lax.psum(jnp.sum(floats * floats, axis=-1), "tensor")
    inverse_rms = lax.rsqrt(squares / width + EPSILON)
    return jnp.sum(floats * inverse_rms[..., None] * tap_gain, axis=2).astype(jnp.bfloat16)


def slot_matrix(owner_ids, slot_ids, live_tokens, owned, dtype):
    index = owner_ids[:, 0] * owned + slot_ids
    table = lax.all_gather(jnp.stack([index, live_tokens]), "dp", axis=1, tiled=True)
    slots = lax.axis_size("dp") * owned
    chosen = jnp.arange(slots, dtype=jnp.int32)[:, None] == table[0][None, :]
    return chosen.astype(dtype), table[1]


def general_body(feature_cache, owner_ids, slot_ids, live_tokens, tap_gain, key_cotangent, value_cotangent):
    owned, block_len, _, columns = feature_cache.shape
    width = columns * lax.axis_size("tensor")
    united = united_of(feature_cache, tap_gain, width).reshape(owned * block_len, columns)
    everywhere = lax.all_gather(united, "dp", axis=0, tiled=True)
    chosen, live = slot_matrix(owner_ids, slot_ids, live_tokens, owned, jnp.bfloat16)
    joined = jnp.concatenate(
        [
            lax.all_gather(key_cotangent, "tensor", axis=1, tiled=True),
            lax.all_gather(value_cotangent, "tensor", axis=1, tiled=True),
        ],
        axis=1,
    )
    mine = lax.all_to_all(joined, "dp", split_axis=1, concat_axis=0, tiled=True)
    rows = mine.shape[1]
    mine = mine.reshape(-1, block_len, rows)
    mask = jnp.arange(block_len, dtype=jnp.int32)[None, :] < live[:, None]
    mine = jnp.where(mask[:, :, None], mine, jnp.zeros_like(mine)).reshape(-1, block_len * rows)
    by_slot = lax.dot_general(
        chosen, mine, (((1,), (0,)), ((), ())), preferred_element_type=jnp.float32
    ).astype(jnp.bfloat16).reshape(-1, rows)
    return lax.dot_general(
        by_slot, everywhere, (((0,), (0,)), ((), ())), preferred_element_type=jnp.float32
    )


MESH = pl.DeviceIdType.MESH
CHUNK = 256


def line_kernel(
    f_in, gain_in, idx_in, key_in, value_in, out,
    fv, gain, sums, scale, uall, cbuf, select, st, gbuf, stage, idxv,
    usend, urecv, csend, crecv, gsend, grecv, osem, lsem, isend, irecv, fsem, zsend, zrecv, ssend, srecv,
):
    z, c = lax.axis_index("dp"), lax.axis_index("tensor")
    owned, taps, block_len, columns = f_in.shape
    tok, share = key_in.shape
    chunks = columns // CHUNK
    groups = fsem.shape[0]
    group = owned // groups
    sibling, across = c + 1 - 2 * lax.rem(c, 2), lax.rem(c + 2, 4)
    across_sibling = lax.rem(sibling + 2, 4)
    is_hub = (z == 1) | (z == 2)

    def remote(src, dst, ss, rs, dz, dc):
        return pltpu.make_async_remote_copy(
            src_ref=src, dst_ref=dst, send_sem=ss, recv_sem=rs,
            device_id={"dp": dz, "tensor": dc}, device_id_type=MESH,
        )

    def cols(j):
        return pl.ds(pl.multiple_of(j * CHUNK, CHUNK), CHUNK)

    def place(owner):
        return pl.ds(pl.multiple_of(owner * tok, tok), tok)

    def f_copy(g):
        part = pl.ds(g * group, group)
        return pltpu.make_async_copy(f_in.at[part], fv.at[part], fsem.at[g])

    own_idx = pltpu.make_async_copy(idx_in, idxv.at[z], lsem.at[1])
    own_gain = pltpu.make_async_copy(gain_in, gain, lsem.at[2])
    for g in range(groups):
        f_copy(g).start()
    own_idx.start()
    own_gain.start()

    @pl.when(z == 1)
    def _():
        pltpu.make_async_copy(key_in, cbuf.at[c, place(1)], lsem.at[0]).start()

    @pl.when(z == 2)
    def _():
        pltpu.make_async_copy(value_in, cbuf.at[c, place(2)], lsem.at[0]).start()

    barrier = pltpu.get_barrier_semaphore()
    for step in range(1, 4):
        pl.semaphore_signal(
            barrier, inc=1, device_id={"dp": lax.rem(z + step, 4), "tensor": c}, device_id_type=MESH
        )
    for step in range(1, 4):
        pl.semaphore_signal(
            barrier, inc=1, device_id={"dp": z, "tensor": lax.rem(c + step, 4)}, device_id_type=MESH
        )
    pl.semaphore_wait(barrier, 6)

    def u_copy(owner, j, sem, dz):
        return remote(uall.at[owner, :, cols(j)], uall.at[owner, :, cols(j)], sem, urecv.at[owner, j], dz, c)

    def idx_copy(owner, sem, dz):
        return remote(idxv.at[owner], idxv.at[owner], sem, irecv.at[owner], dz, c)

    def g_copy(j, dz):
        return remote(stage.at[:, cols(j)], gbuf.at[:, cols(j)], gsend.at[j], grecv.at[j], dz, c)

    def z_copy(ref, n, owner, dz):
        return remote(ref, cbuf.at[c, place(owner)], zsend.at[n], zrecv.at[owner], dz, c)

    def c_copy(kind, owner, who, dc):
        part = cbuf.at[who, place(owner)]
        return remote(part, part, csend.at[kind, owner], crecv.at[kind, owner], z, dc)

    def s_copy(owner, step):
        return remote(
            sums.at[owner], sums.at[owner], ssend.at[step - 1], srecv.at[owner], z, lax.rem(c + step, 4)
        )

    @pl.when(z != 1)
    def _():
        z_copy(key_in, 0, z, 1).start()

    @pl.when(z != 2)
    def _():
        z_copy(value_in, 1, z, 2).start()

    own_idx.wait()

    @pl.when(is_hub)
    def _():
        idx_copy(z, isend.at[0], 3 - z).start()
        pltpu.make_async_copy(key_in, cbuf.at[c, place(z)], lsem.at[0]).wait()
        c_copy(0, z, c, across).start()
        c_copy(1, z, c, sibling).start()

    @pl.when(jnp.logical_not(is_hub))
    def _():
        for n in range(2):
            idx_copy(z, isend.at[n], 1 + n).start()

    width = sums.shape[2]
    lanes = lax.broadcasted_iota(jnp.int32, (block_len, width), 1)
    total = jnp.zeros((block_len, width), jnp.float32)
    for g in range(groups):
        f_copy(g).wait()

        def squares(i, acc, g=g):
            b = g * group + i
            x = fv[b].astype(jnp.float32)
            row = jnp.sum(x * x, axis=-1, keepdims=True)
            for t in range(taps):
                acc = jnp.where(lanes == b * taps + t, row[t], acc)
            return acc

        total = lax.fori_loop(0, group, squares, total, unroll=2)
    sums[c] = total
    for step in range(1, 4):
        s_copy(c, step).start()
    own_gain.wait()
    for step in range(1, 4):
        s_copy(lax.rem(c + step, 4), step).wait_recv()
    inverse = lax.rsqrt((sums[0] + sums[1] + sums[2] + sums[3]) / (4 * columns) + EPSILON)

    def spread(k, carry):
        one = jnp.sum(jnp.where(lanes == k, inverse, 0.0), axis=-1, keepdims=True)
        scale[k] = jnp.broadcast_to(one, (block_len, 128))
        return carry

    lax.fori_loop(0, owned * taps, spread, 0, unroll=8)

    target = 1 + lax.rem(z, 2)

    def unite(j, carry):
        gains = [jnp.broadcast_to(gain[t:t + 1, cols(j)], (block_len, CHUNK)) for t in range(taps)]

        def pair(i, inner):
            rows = []
            for d in range(2):
                b = 2 * i + d
                row = jnp.zeros((block_len, CHUNK), jnp.float32)
                for t in range(taps):
                    s = scale[b * taps + t]
                    s = jnp.concatenate([s] * (CHUNK // 128), axis=-1)
                    row = row + fv[b, t, :, cols(j)].astype(jnp.float32) * s * gains[t]
                rows.append(row)
            where = pl.ds(pl.multiple_of(i * 2 * block_len, 2 * block_len), 2 * block_len)
            uall[z, where, cols(j)] = jnp.concatenate(rows, axis=0).astype(jnp.bfloat16)
            return inner

        lax.fori_loop(0, owned // 2, pair, 0, unroll=4)
        u_copy(z, j, usend.at[0, j], target).start()
        return carry

    lax.fori_loop(0, chunks, unite, 0)

    @pl.when(jnp.logical_not(is_hub))
    def _():
        def out_copy(j):
            return pltpu.make_async_copy(gbuf.at[:, cols(j)], out.at[:, cols(j)], osem.at[j])

        def take(j, carry):
            g_copy(j, target).wait_recv()
            out_copy(j).start()
            return carry

        lax.fori_loop(0, chunks, take, 0)
        for n in range(2):
            idx_copy(z, isend.at[n], 1 + n).wait_send()
        for j in range(chunks):
            out_copy(j).wait()

    @pl.when(is_hub)
    def _():
        leaf, other = 3 * (z - 1), 3 - z
        far_leaf = 3 - leaf
        guests = (leaf, other, far_leaf)

        def out_copy(j):
            return pltpu.make_async_copy(gbuf.at[:, cols(j)], out.at[:, cols(j)], osem.at[j])

        for owner in guests:
            z_copy(key_in, 0, owner, other).wait_recv()
            c_copy(0, owner, c, across).start()
            c_copy(1, owner, c, sibling).start()
        for owner in guests:
            idx_copy(owner, isend.at[0], other).wait_recv()

        def fill(s, carry):
            rows = lax.broadcasted_iota(jnp.int32, (tok, tok), 0) + s * tok
            for k in range(4):
                hit = idxv[k][0:1, :] == rows
                select[place(s), k * tok:(k + 1) * tok] = jnp.where(hit, 1.0, 0.0).astype(jnp.bfloat16)
            return carry

        lax.fori_loop(0, 4, fill, 0)
        for owner in (z,) + guests:
            c_copy(0, owner, across, across).wait_recv()
            c_copy(2, owner, across, sibling).start()

        def hand_on(j):
            u_copy(leaf, j, usend.at[1, j], other).wait_recv()
            u_copy(leaf, j, usend.at[1, j], other).start()

        for owner in range(4):
            c_copy(1, owner, sibling, sibling).wait_recv()
        for owner in range(4):
            c_copy(2, owner, across_sibling, sibling).wait_recv()

        def by_slot(k, carry):
            st[k // 2, pl.ds(pl.multiple_of(lax.rem(k, 2) * share, share), share), :] = lax.dot_general(
                cbuf[k], select[...], (((0,), (1,)), ((), ())), preferred_element_type=jnp.float32
            ).astype(jnp.bfloat16)
            for step in range(chunks // 4):
                hand_on(k * (chunks // 4) + step)
            return carry

        lax.fori_loop(0, 4, by_slot, 0)

        def finish(j, carry):
            u_copy(other, j, usend.at[0, j], other).wait_recv()
            u_copy(far_leaf, j, usend.at[0, j], other).wait_recv()
            part = uall[:, :, cols(j)].reshape(4 * tok, CHUNK)
            stage[:, cols(j)] = jnp.dot(st[z - 1], part, preferred_element_type=jnp.float32).astype(jnp.bfloat16)
            g_copy(j, leaf).start()
            gbuf[:, cols(j)] = jnp.dot(st[2 - z], part, preferred_element_type=jnp.float32).astype(jnp.bfloat16)
            out_copy(j).start()
            return carry

        lax.fori_loop(0, chunks, finish, 0)
        idx_copy(z, isend.at[0], other).wait_send()
        for owner in range(4):
            c_copy(0, owner, c, across).wait_send()
            c_copy(1, owner, c, sibling).wait_send()
            c_copy(2, owner, across, sibling).wait_send()
        for j in range(chunks):
            u_copy(leaf, j, usend.at[1, j], other).wait_send()
            g_copy(j, leaf).wait_send()
            out_copy(j).wait()

    for step in range(1, 4):
        s_copy(c, step).wait_send()
    for j in range(chunks):
        u_copy(z, j, usend.at[0, j], target).wait_send()

    @pl.when(z != 1)
    def _():
        z_copy(key_in, 0, z, 1).wait_send()

    @pl.when(z != 2)
    def _():
        z_copy(value_in, 1, z, 2).wait_send()


def line_body(feature_cache, owner_ids, slot_ids, live_tokens, tap_gain, key_cotangent, value_cotangent):
    owned, block_len, taps, columns = feature_cache.shape
    tok, share = key_cotangent.shape
    chunks = columns // CHUNK
    offsets = jnp.arange(block_len, dtype=jnp.int32)
    first = (owner_ids[:, 0] * owned + slot_ids) * block_len
    index = jnp.where(offsets[None, :] < live_tokens[:, None], first[:, None] + offsets[None, :], -1)
    index = jnp.broadcast_to(index.reshape(1, tok), (8, tok))
    features = jnp.transpose(feature_cache, (0, 2, 1, 3))
    anywhere = pl.BlockSpec(memory_space=pl.ANY)
    dma = pltpu.SemaphoreType.DMA
    wide = -(-owned * taps // 128) * 128
    result = pl.pallas_call(
        line_kernel,
        out_shape=jax.ShapeDtypeStruct((tok, columns), jnp.bfloat16),
        in_specs=[anywhere] * 5,
        out_specs=anywhere,
        scratch_shapes=[
            pltpu.VMEM((owned, taps, block_len, columns), jnp.bfloat16),
            pltpu.VMEM((taps, columns), jnp.float32),
            pltpu.VMEM((4, block_len, wide), jnp.float32),
            pltpu.VMEM((owned * taps, block_len, 128), jnp.float32),
            pltpu.VMEM((4, tok, columns), jnp.bfloat16),
            pltpu.VMEM((4, 4 * tok, share), jnp.bfloat16),
            pltpu.VMEM((4 * tok, 4 * tok), jnp.bfloat16),
            pltpu.VMEM((2, 2 * share, 4 * tok), jnp.bfloat16),
            pltpu.VMEM((tok, columns), jnp.bfloat16),
            pltpu.VMEM((tok, columns), jnp.bfloat16),
            pltpu.VMEM((4, 8, tok), jnp.int32),
            dma((2, chunks)), dma((4, chunks)), dma((3, 4)), dma((3, 4)),
            dma((chunks,)), dma((chunks,)), dma((chunks,)), dma((3,)), dma((2,)), dma((4,)),
            dma((8,)), dma((2,)), dma((4,)), dma((3,)), dma((4,)),
        ],
        compiler_params=pltpu.CompilerParams(
            collective_id=0, has_side_effects=True, vmem_limit_bytes=58 * 1024 * 1024
        ),
    )(features, tap_gain, index, key_cotangent, value_cotangent)
    return result.astype(jnp.float32)


def solution(mesh):
    in_specs = (
        P(("groups", "dp"), None, None, "tensor"),
        P(("groups", "dp"), None),
        P(("groups", "dp")),
        P(("groups", "dp")),
        P(None, "tensor"),
        P(("groups", "dp"), "tensor"),
        P(("groups", "dp"), "tensor"),
    )
    body = line_body if mesh.shape["dp"] == 4 and mesh.shape["tensor"] == 4 else general_body
    out_specs = P(("groups", "dp"), "tensor")
    return jax.shard_map(body, mesh=mesh, in_specs=in_specs, out_specs=out_specs, check_vma=False)
```

time: 142 us -> 125 us (0.88)
  Pallas kernels: 104 us -> 119 us
  blocking collectives: 10.6 us -> 0 us
  starting transfers between devices: 8.06 us -> 0 us
  other arithmetic: 12.8 us -> 5.54 us
  local copies, waits for them, and re-layouts: 5.86 us -> 0.7 us
    pallas_call x1, Pallas kernels: 104 us -> 119 us  [line_body(): pl.pallas_call(line_kernel, out_shape=jax.ShapeDtypeStruct((tok, columns)...]
    reduce_sum x2 -> x0, other arithmetic: 10.9 us -> none  [the longest x1 6.82 us: united_of(): jnp.sum(floats * inverse_rms[..., None] * tap_gain, axis=2)]
    psum x1 -> x0, blocking collectives: 10.6 us -> none  [united_of(): squares = lax.psum(jnp.sum(floats * floats, axis=-1), 'tensor')]
    ppermute x3 -> x0, starting transfers between devices: 8.06 us -> none  [the longest x1 5.94 us: line_body(): lax.ppermute(jnp.where(z == 3, key_cotangent, value_cotangent), 'dp', [(0...]
    unnamed x15 -> x0, local copies, waits for them, and re-layouts: 4.88 us -> none
    convert_element_type x0 -> x1, other arithmetic: none -> 4.13 us  [line_body(): return result.astype(jnp.float32)]
    select_n x1 -> x0, other arithmetic: 1.8 us -> none  [line_body(): jnp.where(z == 3, key_cotangent, value_cotangent)]
  transfers between devices with their start and end apart: 3 -> 0, of which waited for: 0 -> 0; matrix products, arithmetic and copies ran while one was open for 8% -> 0% of each run, Pallas kernels for 0% -> 0%
where the time goes in v3:
time: 125 us
  Pallas kernels  119 us (95%)
  other arithmetic  5.54 us (4%)
    pallas_call x1, Pallas kernels, line_body(): pl.pallas_call(line_kernel, out_shape=jax.ShapeDtypeStruct((tok, columns)...  119 us
    convert_element_type x1, other arithmetic, line_body(): return result.astype(jnp.float32)  4.13 us

profile of v3, /device:TPU:0, one launch (start us, length us, event | category | flops | bytes accessed | tf_op | source)
XLA Modules:
  0.0 124.8 jit_solution(13407013624713804419)
XLA Ops:
  0.0 0.7 fusion
  0.7 0.7 add_select_fusion
  1.4 0.1 select_n.12
  1.5 0.6 broadcast_in_dim.7.idx_in
  2.1 118.6 %shard_map.73 = bf16[512,2048]{1,0:T(8,128)(2,1)} custom-call(bf16[64,3,8,2048]{3,2,1,0:T(8,128)(2,1)} %bitcast.5, f32[3,2048]{1,0:T(4,128)} %gain_in.1, s32[8,512]{1,0:T(8,128)} %broadcast_in_dim.7.idx_in, bf16[512,256]{1,0:T(8,128)(2,1)} %key_in.1, bf16[512,256]{1,0:T(8,128)(2,1)} %value_in.1), custom_call_target="tpu_custom_call" | custom-call | tf_op jit(solution)/shard_map/pallas_call | solution.py:321
  120.7 4.1 %convert_element_type.3 = f32[512,2048]{1,0:T(8,128)} convert(bf16[512,2048]{1,0:T(8,128)(2,1)} %shard_map.73) | non-fusion elementwise | flops 1048576 | bytes 6291456 | tf_op jit(solution)/shard_map/convert_element_type | solution.py:346

commit v4 on v3

--- a/solution.py
+++ b/solution.py
@@ -50,11 +50,11 @@
 
 
 MESH = pl.DeviceIdType.MESH
-CHUNK = 256
+CHUNK = 128
 
 
 def line_kernel(
-    f_in, gain_in, idx_in, key_in, value_in, out,
+    f_in, gain_in, owner_in, slot_in, live_in, key_in, value_in, out,
     fv, gain, sums, scale, uall, cbuf, select, st, gbuf, stage, idxv,
     usend, urecv, csend, crecv, gsend, grecv, osem, lsem, isend, irecv, fsem, zsend, zrecv, ssend, srecv,
 ):
@@ -84,11 +84,9 @@
         part = pl.ds(g * group, group)
         return pltpu.make_async_copy(f_in.at[part], fv.at[part], fsem.at[g])
 
-    own_idx = pltpu.make_async_copy(idx_in, idxv.at[z], lsem.at[1])
     own_gain = pltpu.make_async_copy(gain_in, gain, lsem.at[2])
     for g in range(groups):
         f_copy(g).start()
-    own_idx.start()
     own_gain.start()
 
     @pl.when(z == 1)
@@ -139,7 +137,19 @@
     def _():
         z_copy(value_in, 1, z, 2).start()
 
-    own_idx.wait()
+    listed = owner_in.shape[1]
+    sub = lax.broadcasted_iota(jnp.int32, (8, listed), 0)
+    entry = owner_in[...] * owned + slot_in[...]
+    both = jnp.where(sub == 0, jnp.broadcast_to(entry, (8, listed)), jnp.broadcast_to(live_in[...], (8, listed)))
+    start = lax.broadcasted_iota(jnp.int32, (listed, tok), 0) * block_len
+    token = lax.broadcasted_iota(jnp.int32, (listed, tok), 1)
+    inside = jnp.where((token >= start) & (token < start + block_len), 1.0, 0.0)
+    wide = jnp.dot(
+        both.astype(jnp.float32), inside, precision=lax.Precision.HIGHEST, preferred_element_type=jnp.float32
+    ).astype(jnp.int32)
+    offset = lax.rem(lax.broadcasted_iota(jnp.int32, (1, tok), 1), block_len)
+    index = jnp.where(offset < wide[1:2], wide[0:1] * block_len + offset, -1)
+    idxv[z] = jnp.broadcast_to(index, (8, tok))
 
     @pl.when(is_hub)
     def _():
@@ -310,10 +320,6 @@
     owned, block_len, taps, columns = feature_cache.shape
     tok, share = key_cotangent.shape
     chunks = columns // CHUNK
-    offsets = jnp.arange(block_len, dtype=jnp.int32)
-    first = (owner_ids[:, 0] * owned + slot_ids) * block_len
-    index = jnp.where(offsets[None, :] < live_tokens[:, None], first[:, None] + offsets[None, :], -1)
-    index = jnp.broadcast_to(index.reshape(1, tok), (8, tok))
     features = jnp.transpose(feature_cache, (0, 2, 1, 3))
     anywhere = pl.BlockSpec(memory_space=pl.ANY)
     dma = pltpu.SemaphoreType.DMA
@@ -321,7 +327,7 @@
     result = pl.pallas_call(
         line_kernel,
         out_shape=jax.ShapeDtypeStruct((tok, columns), jnp.bfloat16),
-        in_specs=[anywhere] * 5,
+        in_specs=[anywhere] * 2 + [pl.BlockSpec(memory_space=pltpu.VMEM)] * 3 + [anywhere] * 2,
         out_specs=anywhere,
         scratch_shapes=[
             pltpu.VMEM((owned, taps, block_len, columns), jnp.bfloat16),
@@ -342,7 +348,15 @@
         compiler_params=pltpu.CompilerParams(
             collective_id=0, has_side_effects=True, vmem_limit_bytes=58 * 1024 * 1024
         ),
-    )(features, tap_gain, index, key_cotangent, value_cotangent)
+    )(
+        features,
+        tap_gain,
+        owner_ids.reshape(1, -1),
+        slot_ids.reshape(1, -1),
+        live_tokens.reshape(1, -1),
+        key_cotangent,
+        value_cotangent,
+    )
     return result.astype(jnp.float32)
 
 

time: 125 us -> 121 us (0.968)
  Pallas kernels: 119 us -> 117 us
  other arithmetic: 5.54 us -> 4.13 us
    pallas_call x1, Pallas kernels: 119 us -> 117 us  [line_body(): pl.pallas_call(line_kernel, out_shape=jax.ShapeDtypeStruct((tok, columns)...]
where the time goes in v4:
time: 121 us
  Pallas kernels  117 us (97%)
  other arithmetic  4.13 us (3%)
    pallas_call x1, Pallas kernels, line_body(): pl.pallas_call(line_kernel, out_shape=jax.ShapeDtypeStruct((tok, columns)...  117 us
    convert_element_type x1, other arithmetic, line_body(): return result.astype(jnp.float32)  4.13 us

profile of v4, /device:TPU:0, one launch (start us, length us, event | category | flops | bytes accessed | tf_op | source)
XLA Modules:
  0.0 121.1 jit_solution(11725996410450643967)
XLA Ops:
  0.0 117.0 %shard_map.73 = bf16[512,2048]{1,0:T(8,128)(2,1)} custom-call(bf16[64,3,8,2048]{3,2,1,0:T(8,128)(2,1)} %bitcast.4, f32[3,2048]{1,0:T(4,128)} %gain_in.1, s32[1,64]{1,0:T(1,128)} %bitcast.5, s32[1,64]{1,0:T(1,128)} %bitcast.6, s32[1,64]{1,0:T(1,128)} %bitcast.7, bf16[512,256]{1,0:T(8,128)(2,1)} %key_in.1, bf16[512,256]{1,0:T(8,128)(2,1)} %value_in.1), custom_call_target="tpu_custom_call" | custom-call | tf_op jit(solution)/shard_map/pallas_call | solution.py:327
  117.0 4.1 %convert_element_type.3 = f32[512,2048]{1,0:T(8,128)} convert(bf16[512,2048]{1,0:T(8,128)(2,1)} %shard_map.73) | non-fusion elementwise | flops 1048576 | bytes 6291456 | tf_op jit(solution)/shard_map/convert_element_type | solution.py:360
